TPU v7x, 128 devices: a whole 4x4x4 slice. The times are simulated.
128 devices in a mesh: row: 4 (over y), col: 32 (over x, z, core).
Axes of the slice: x: 4, y: 4, z: 4, core: 2. Of those that a mesh axis runs over, the one named last changes fastest.
Arguments:
- coordinates: float32 [3, 65536], replicated, may hold values from 0 to 1
- ordering: int32 [65536], replicated, may hold values from 0 to 65535, each once
- neighbours: int32 [256, 4], replicated, may hold values from 0 to 254, as said below
- cross: float32 [256, 4, 256, 256], P(('row', 'col')), may hold values from -0.1875 to 0.1875
- whitening: float32 [256, 256, 256], P(('row', 'col')), may hold values from -0.1875 to 0.1875
- solution: float32 [256, 8, 256], P(('row', 'col')), may hold values from -6 to 6
- residual: float32 [256, 8, 256], P(('row', 'col')), may hold values from -40 to 40
- direction: float32 [256, 8, 256], P(('row', 'col')), may hold values from -40 to 40
Outputs:
- solution_next: float32 [256, 8, 256], P(('row', 'col'))
- residual_next: float32 [256, 8, 256], P(('row', 'col'))
- direction_next: float32 [256, 8, 256], P(('row', 'col'))
Inputs may be any that keep to these rules, and one draw needn't show every extreme that they name: `neighbours`: row b lists b - 1 first, then further distinct blocks below b - 1; where fewer than 4 earlier blocks exist the remaining entries equal b itself.
All inputs are finite; a program needn't handle non-finite values.
Results may differ from a plain program's by a relative error of at most 0.00023.
Values sent between devices are 32-bit elements; how exact they have to be, the bound alone decides.
No kernel may reach another device: no remote copies, remote signals or barrier semaphores. Data moves between devices by JAX's collectives and lax.ppermute only.
A program may use at most 192 MiB of HBM per device.

v0:
```python
import math
import jax
import jax.numpy as jnp
from jax import lax
from jax.sharding import PartitionSpec as P

kernel_rate = math.sqrt(3.0) / 0.3
variance = 0.05
nugget = 1.0
highest = lax.Precision.HIGHEST


def covariance(rows, columns):
    apart_x = rows[0][:, None] - columns[0][None, :]
    apart_y = rows[1][:, None] - columns[1][None, :]
    apart_z = rows[2][:, None] - columns[2][None, :]
    distance = jnp.sqrt(apart_x * apart_x + apart_y * apart_y + apart_z * apart_z)
    scaled = kernel_rate * distance
    return variance * (1.0 + scaled) * jnp.exp(-scaled)


def per_device(coordinates, ordering, neighbours, cross, whitening, solution, residual, direction):
    own_blocks = residual.shape[0]
    rhs_count = residual.shape[1]
    block_size = residual.shape[2]
    total_blocks = ordering.shape[0] // block_size
    points = coordinates[:, ordering].reshape(3, total_blocks, block_size)
    device = lax.axis_index(("row", "col"))
    first_block = device * own_blocks
    own_ids = first_block + jnp.arange(own_blocks, dtype=jnp.int32)
    own_lists = lax.dynamic_slice_in_dim(neighbours, first_block, own_blocks, 0)
    is_earlier = own_lists < own_ids[:, None]
    valid = is_earlier.astype(jnp.float32)
    whiten = whitening + jnp.eye(block_size, dtype=jnp.float32)[None]

    def selector(count):
        inside = (own_lists >= 0) & (own_lists < count) & is_earlier
        matches = own_lists[:, :, None] == jnp.arange(count, dtype=jnp.int32)[None, None, :]
        return (matches & inside[:, :, None]).astype(jnp.float32)

    def precondition(field):
        piece = lax.all_gather(field, ("row", "col"), axis=0, tiled=True)
        picks = selector(piece.shape[0])
        near = jnp.einsum("bkm,mcj->bkcj", picks, piece, precision=highest)
        lowered = field - jnp.einsum("bkcj,bkij->bci", near, cross, precision=highest)
        mapped = jnp.einsum("bcj,bij->bci", lowered, whiten, precision=highest)
        scaled = jnp.einsum("bci,bij->bcj", mapped, whiten, precision=highest)
        spread = (
            jnp.einsum("bci,bkij->bkcj", scaled, cross, precision=highest) * valid[:, :, None, None]
        )
        picks = selector(own_blocks * lax.axis_size(("row", "col")))
        back = lax.psum_scatter(
            jnp.einsum("bkm,bkcj->mcj", picks, spread, precision=highest),
            ("row", "col"),
            scatter_dimension=0,
            tiled=True,
        )
        return scaled - back

    own_points = lax.dynamic_slice_in_dim(points, first_block, own_blocks, 1).reshape(
        3, own_blocks * block_size
    )
    start_sum = jnp.zeros((rhs_count, own_blocks * block_size), jnp.float32)
    piece = lax.all_gather(direction, ("row", "col"), axis=0, tiled=True)
    span = piece.shape[0]
    group = math.gcd(span, 16)

    def one_group(index, running):
        begin = (index * group).astype(jnp.int32)
        column_points = lax.dynamic_slice_in_dim(points, begin, group, 1).reshape(
            3, group * block_size
        )
        column_field = (
            lax.dynamic_slice_in_dim(piece, begin, group, 0)
            .transpose(1, 0, 2)
            .reshape(rhs_count, group * block_size)
        )
        tile = covariance(own_points, column_points)
        return running + lax.dot_general(
            column_field, tile, (((1,), (1,)), ((), ())), precision=highest
        )

    image_flat = lax.fori_loop(0, span // group, one_group, start_sum)
    image = (
        image_flat.reshape(rhs_count, own_blocks, block_size).transpose(1, 0, 2)
        + nugget * direction
    )
    pre = precondition(residual)
    old, curvature = lax.psum(
        (jnp.sum(residual * pre, axis=(0, 2)), jnp.sum(direction * image, axis=(0, 2))),
        ("row", "col"),
    )
    step_size = (old / curvature)[None, :, None]
    solution_next = solution + step_size * direction
    residual_next = residual - step_size * image
    pre_next = precondition(residual_next)
    newer = lax.psum(jnp.sum(residual_next * pre_next, axis=(0, 2)), ("row", "col"))
    ratio = (newer / old)[None, :, None]
    direction_next = pre_next + ratio * direction
    return (solution_next, residual_next, direction_next)


def solution(mesh):
    placed = (
        P(),
        P(),
        P(),
        P(("row", "col"), None, None, None),
        P(("row", "col"), None, None),
        P(("row", "col"), None, None),
        P(("row", "col"), None, None),
        P(("row", "col"), None, None),
    )
    return jax.shard_map(
        per_device,
        mesh=mesh,
        in_specs=placed,
        out_specs=(
            P(("row", "col"), None, None),
            P(("row", "col"), None, None),
            P(("row", "col"), None, None),
        ),
        check_vma=False,
    )
```

profile of v0, /device:TPU:1, one launch (start us, length us, event | category | flops | bytes accessed | tf_op | source)
XLA Modules:
  0.0 1771.8 jit_solution(8504843684024733289)
XLA Ops:
  9.8 16.2 copy.23
  26.1 226.5 %gather_fusion = f32[65536,3]{1,0:T(8,128)} fusion(f32[3,65536]{0,1:T(8,128)} %copy.23, s32[65536]{0:T(1024)S(1)} %fusion.45), kind=kCustom, calls=%fused_computation | custom fusion | bytes 1835008 | tf_op jit(solution)/shard_map/gather | solution.py:27
  252.6 19.6 %copy.25 = f32[3,256,256]{2,1,0:T(8,128)} copy(f32[3,256,256]{0,2,1:T(8,128)} %bitcast.94) | data formatting | bytes 1572864
  284.0 223.9 %while.14 = (s32[]{:T(128)}, f32[8,512]{1,0:T(8,128)S(1)}, f32[256,8,256]{2,1,0:T(8,128)}, f32[3,512]{1,0:T(4,128)S(1)}, f32[3,256,256]{2,1,0:T(8,128)}, /*index...) while((s32[]{:T(128)}, f32[8,512]{1,0:T(8,128)S(1)}, ...), condition=%wide.region_4.0_spmd.clone, body=%wide.region_3.0_spmd.clone.sunk | while | flops 228597760 | bytes 690381 | solution.py:83
  285.8 12.2 fusion.88
  299.8 12.2 fusion.88
  313.8 12.2 fusion.88
  327.8 12.2 fusion.88
  341.8 12.2 fusion.88
  355.8 12.2 fusion.88
  369.8 12.2 fusion.88
  383.8 12.2 fusion.88
  397.8 12.2 fusion.88
  411.8 12.2 fusion.88
  425.8 12.2 fusion.88
  439.7 12.2 fusion.88
  453.7 12.2 fusion.88
  467.7 12.2 fusion.88
  481.7 12.2 fusion.88
  508.1 412.1 %reduce-scatter.3.cloned.1.call-done = f32[2,8,256]{2,1,0:T(8,128)} async-done(((f32[256,8,256]{2,1,0:T(8,128)}), f32[2,8,256]{2,1,0:T(8,128)}) %reduce-scatter.3.cloned.1.call-update) | async-done | bytes 16400 | tf_op jit(solution)/shard_map/reduce_scatter | solution.py:52
  921.0 69.2 %all-reduce = (f32[8]{0:T(128)S(1)}, f32[8]{0:T(128)S(1)}) all-reduce(f32[8]{0:T(128)S(1)} %multiply_reduce_fusion.2, f32[8]{0:T(128)S(1)} %get-tuple-element.140), channel_id=1, replica_groups=mesh['row'=4,'col'=32] {'row','col'}, use_global_device_ids=true, to_apply=%region_2.0 | all-reduce | flops 16 | bytes 128 | tf_op jit(solution)/shard_map/psum | solution.py:89
  991.2 62.0 %all-gather.8.cloned.1.call-done = f32[256,8,256]{2,1,0:T(8,128)} async-done(((f32[2,8,256]{2,1,0:T(8,128)}), f32[256,8,256]{2,1,0:T(8,128)}) %all-gather.8.cloned.1.call-update) | async-done | bytes 2097168 | tf_op jit(solution)/shard_map/all_gather | solution.py:42
  1064.3 630.2 %reduce-scatter.5.cloned.1.call-done = f32[2,8,256]{2,1,0:T(8,128)} async-done(((f32[256,8,256]{2,1,0:T(8,128)}), f32[2,8,256]{2,1,0:T(8,128)}) %reduce-scatter.5.cloned.1.call-update) | async-done | bytes 16400 | tf_op jit(solution)/shard_map/reduce_scatter | solution.py:52
  1695.3 69.2 %psum.23 = f32[8]{0:T(128)S(1)} all-reduce(f32[8]{0:T(128)S(1)} %get-tuple-element.138), channel_id=1, replica_groups=mesh['row'=4,'col'=32] {'row','col'}, use_global_device_ids=true, to_apply=%region_9.0 | all-reduce | flops 8 | bytes 64 | tf_op jit(solution)/shard_map/psum | solution.py:97
  (155 shorter events, 69.2 us)
Async XLA Ops:
  7.2 269.0 %copy-start = (f32[2,4,256,256]{3,2,1,0:T(8,128)S(1)}, f32[2,4,256,256]{3,2,1,0:T(8,128)}, u32[]{:S(2)}) copy-start(f32[2,4,256,256]{3,2,1,0:T(8,128)} %param.13) | copy-start | bytes 6291460
  7.2 266.1 %all-gather.4.cloned.1.call-start = ((), (), s32[]{:S(2)}) async-start(), calls=%async_computation.2 | async-start | bytes 2113536 | tf_op jit(solution)/shard_map/all_gather | solution.py:42
  7.9 276.1 %all-gather.6.cloned.1.call-start = ((), (), s32[]{:S(2)}) async-start(), calls=%async_computation.4 | async-start | bytes 2113536 | tf_op jit(solution)/shard_map/all_gather | solution.py:64
  8.7 911.5 %reduce-scatter.3.cloned.1.call-start = ((), (), s32[]{:S(2)}) async-start(), calls=%async_computation.3 | async-start | bytes 2113536 | tf_op jit(solution)/shard_map/reduce_scatter | solution.py:52
  9.8 16.2 copy-start.4
  252.6 23.6 %copy-start.2 = (f32[2,8,256]{2,1,0:T(8,128)S(1)}, f32[2,8,256]{2,1,0:T(8,128)}, u32[]{:S(2)}) copy-start(f32[2,8,256]{2,1,0:T(8,128)} %param.16) | copy-start | bytes 49156
  252.6 25.5 %copy-start.1 = (f32[2,256,256]{2,1,0:T(8,128)S(1)}, f32[2,256,256]{2,1,0:T(8,128)}, u32[]{:S(2)}) copy-start(f32[2,256,256]{2,1,0:T(8,128)} %param.14) | copy-start | bytes 1572868
  283.8 769.4 %all-gather.8.cloned.1.call-start = ((), (), s32[]{:S(2)}) async-start(), calls=%async_computation.5 | async-start | bytes 2113536 | tf_op jit(solution)/shard_map/all_gather | solution.py:42
  284.0 224.0 %copy-start.5 = (f32[2,8,256]{2,1,0:T(8,128)S(1)}, f32[2,8,256]{2,1,0:T(8,128)}, u32[]{:S(2)}) copy-start(f32[2,8,256]{2,1,0:T(8,128)} %param.17) | copy-start | bytes 49156
  990.2 774.4 %copy-start.6 = (f32[2,8,256]{2,1,0:T(8,128)S(1)}, f32[2,8,256]{2,1,0:T(8,128)}, u32[]{:S(2)}) copy-start(f32[2,8,256]{2,1,0:T(8,128)} %param.15) | copy-start | bytes 49156
  990.9 703.6 %copy-start.3 = (f32[2,8,256]{2,1,0:T(8,128)S(1)}, f32[2,8,256]{2,1,0:T(8,128)}, u32[]{:S(2)}) copy-start(f32[2,8,256]{2,1,0:T(8,128)} %multiply_subtract_fusion) | copy-start | bytes 49156
  990.9 703.6 %reduce-scatter.5.cloned.1.call-start = ((), (), s32[]{:S(2)}) async-start(), calls=%async_computation.6 | async-start | bytes 2113536 | tf_op jit(solution)/shard_map/reduce_scatter | solution.py:52
Sparse Core Ops, SparseCore 0:
  11.2 68.9 all-gather.3
  83.3 62.7 all-gather.5
  283.9 636.2 reduce-scatter.2
  991.0 62.0 all-gather.7
  1064.4 630.0 reduce-scatter.4
where the time goes:
time: 1780 us; the launch traced here: 1770 us
  waiting for transfers between devices  1110 us (62%)
  local copies, waits for them, and re-layouts  297 us (17%)
  matrix products  212 us (12%)
  blocking collectives  138 us (8%)
    reduce_scatter x2, waiting for transfers between devices, precondition(): lax.psum_scatter(jnp.einsum('bkm,bkcj->mcj', picks, spread, precision=hig...  1040 us
    gather x1, local copies, waits for them, and re-layouts, per_device(): points = coordinates[:, ordering].reshape(3, total_blocks, block_size)  226 us
    dot_general x16, matrix products, one_group(): lax.dot_general(column_field, tile, (((1,), (1,)), ((), ())), precision=h...  195 us
    psum x1, blocking collectives, per_device(): lax.psum(jnp.sum(residual_next * pre_next, axis=(0, 2)), ('row', 'col'))  69.2 us
    psum x1, blocking collectives, per_device(): lax.psum((jnp.sum(residual * pre, axis=(0, 2)), jnp.sum(direction * image...  69.2 us
    all_gather x2, waiting for transfers between devices, precondition(): piece = lax.all_gather(field, ('row', 'col'), axis=0, tiled=True)  62 us
    unnamed x16, local copies, waits for them, and re-layouts  35.9 us
  transfers between devices with their start and end apart: 5, of which 3 were waited for; matrix products, arithmetic and copies ran while one was open for 28% of the time, Pallas kernels for 0%

commit v1 on v0

--- a/solution.py
+++ b/solution.py
@@ -87,8 +87,10 @@
     )
     pre = precondition(residual)
     old, curvature = lax.psum(
-        (jnp.sum(residual * pre, axis=(0, 2)), jnp.sum(direction * image, axis=(0, 2))),
-        ("row", "col"),
+        lax.psum(
+            (jnp.sum(residual * pre, axis=(0, 2)), jnp.sum(direction * image, axis=(0, 2))), "row"
+        ),
+        "col",
     )
     step_size = (old / curvature)[None, :, None]
     solution_next = solution + step_size * direction

time: 1780 us -> 1780 us (level)
    psum x0 -> x1, blocking collectives: none -> 71.1 us  [per_device(): lax.psum(lax.psum((jnp.sum(residual * pre, axis=(0, 2)), jnp.sum(directio...]
    psum x1, blocking collectives: 69.2 us -> 6.15 us  [per_device(): lax.psum((jnp.sum(residual * pre, axis=(0, 2)), jnp.sum(direction * image...]
where the time goes in v1:
time: 1780 us
  waiting for transfers between devices  1100 us (62%)
  local copies, waits for them, and re-layouts  296 us (17%)
  matrix products  212 us (12%)
  blocking collectives  146 us (8%)
    reduce_scatter x2, waiting for transfers between devices, precondition(): lax.psum_scatter(jnp.einsum('bkm,bkcj->mcj', picks, spread, precision=hig...  1040 us
    gather x1, local copies, waits for them, and re-layouts, per_device(): points = coordinates[:, ordering].reshape(3, total_blocks, block_size)  226 us
    dot_general x16, matrix products, one_group(): lax.dot_general(column_field, tile, (((1,), (1,)), ((), ())), precision=h...  195 us
    psum x1, blocking collectives, per_device(): lax.psum(lax.psum((jnp.sum(residual * pre, axis=(0, 2)), jnp.sum(directio...  71.1 us
    psum x1, blocking collectives, per_device(): lax.psum(jnp.sum(residual_next * pre_next, axis=(0, 2)), ('row', 'col'))  69.2 us
    all_gather x2, waiting for transfers between devices, precondition(): piece = lax.all_gather(field, ('row', 'col'), axis=0, tiled=True)  60.9 us
    unnamed x16, local copies, waits for them, and re-layouts  35.9 us
  transfers between devices with their start and end apart: 5, of which 3 were waited for; matrix products, arithmetic and copies ran while one was open for 28% of the time, Pallas kernels for 0%

profile of v1, /device:TPU:1, one launch (start us, length us, event | category | flops | bytes accessed | tf_op | source)
XLA Modules:
  0.0 1778.7 jit_solution(12413722950996858092)
XLA Ops:
  9.8 16.2 copy.23
  26.1 226.1 %gather_fusion = f32[65536,3]{1,0:T(8,128)} fusion(f32[3,65536]{0,1:T(8,128)} %copy.23, s32[65536]{0:T(1024)S(1)} %fusion.45), kind=kCustom, calls=%fused_computation | custom fusion | bytes 1835008 | tf_op jit(solution)/shard_map/gather | solution.py:27
  252.2 19.6 %copy.25 = f32[3,256,256]{2,1,0:T(8,128)} copy(f32[3,256,256]{0,2,1:T(8,128)} %bitcast.94) | data formatting | bytes 1572864
  283.7 223.9 %while.14 = (s32[]{:T(128)}, f32[8,512]{1,0:T(8,128)S(1)}, f32[256,8,256]{2,1,0:T(8,128)}, f32[3,512]{1,0:T(4,128)S(1)}, f32[3,256,256]{2,1,0:T(8,128)}, /*index...) while((s32[]{:T(128)}, f32[8,512]{1,0:T(8,128)S(1)}, ...), condition=%wide.region_5.0_spmd.clone, body=%wide.region_4.0_spmd.clone.sunk | while | flops 228597760 | bytes 690381 | solution.py:83
  285.5 12.2 fusion.88
  299.5 12.2 fusion.88
  313.4 12.2 fusion.88
  327.4 12.2 fusion.88
  341.4 12.2 fusion.88
  355.4 12.2 fusion.88
  369.4 12.2 fusion.88
  383.4 12.2 fusion.88
  397.4 12.2 fusion.88
  411.4 12.2 fusion.88
  425.4 12.2 fusion.88
  439.4 12.2 fusion.88
  453.4 12.2 fusion.88
  467.4 12.2 fusion.88
  481.4 12.2 fusion.88
  507.8 412.3 %reduce-scatter.3.cloned.1.call-done = f32[2,8,256]{2,1,0:T(8,128)} async-done(((f32[256,8,256]{2,1,0:T(8,128)}), f32[2,8,256]{2,1,0:T(8,128)}) %reduce-scatter.3.cloned.1.call-update) | async-done | bytes 16400 | tf_op jit(solution)/shard_map/reduce_scatter | solution.py:52
  927.1 71.1 %all-reduce = (f32[8]{0:T(128)S(1)}, f32[8]{0:T(128)S(1)}) all-reduce(f32[8]{0:T(128)S(1)} %get-tuple-element.138, f32[8]{0:T(128)S(1)} %get-tuple-element.139), channel_id=1, replica_groups=mesh['row'=4,'col'=32] {'col'}, use_global_device_ids=true, to_apply=%region_3.0 | all-reduce | flops 16 | bytes 128 | tf_op jit(solution)/shard_map/psum | solution.py:89
  999.2 60.8 %all-gather.8.cloned.1.call-done = f32[256,8,256]{2,1,0:T(8,128)} async-done(((f32[2,8,256]{2,1,0:T(8,128)}), f32[256,8,256]{2,1,0:T(8,128)}) %all-gather.8.cloned.1.call-update) | async-done | bytes 2097168 | tf_op jit(solution)/shard_map/all_gather | solution.py:42
  1071.2 630.2 %reduce-scatter.5.cloned.1.call-done = f32[2,8,256]{2,1,0:T(8,128)} async-done(((f32[256,8,256]{2,1,0:T(8,128)}), f32[2,8,256]{2,1,0:T(8,128)}) %reduce-scatter.5.cloned.1.call-update) | async-done | bytes 16400 | tf_op jit(solution)/shard_map/reduce_scatter | solution.py:52
  1702.3 69.2 %psum.39 = f32[8]{0:T(128)S(1)} all-reduce(f32[8]{0:T(128)S(1)} %get-tuple-element.140), channel_id=1, replica_groups=mesh['row'=4,'col'=32] {'row','col'}, use_global_device_ids=true, to_apply=%region_11.0 | all-reduce | flops 8 | bytes 64 | tf_op jit(solution)/shard_map/psum | solution.py:99
  (156 shorter events, 75.3 us)
Async XLA Ops:
  7.2 268.7 %copy-start = (f32[2,4,256,256]{3,2,1,0:T(8,128)S(1)}, f32[2,4,256,256]{3,2,1,0:T(8,128)}, u32[]{:S(2)}) copy-start(f32[2,4,256,256]{3,2,1,0:T(8,128)} %param.13) | copy-start | bytes 6291460
  7.2 265.8 %all-gather.4.cloned.1.call-start = ((), (), s32[]{:S(2)}) async-start(), calls=%async_computation.2 | async-start | bytes 2113536 | tf_op jit(solution)/shard_map/all_gather | solution.py:42
  7.9 275.7 %all-gather.6.cloned.1.call-start = ((), (), s32[]{:S(2)}) async-start(), calls=%async_computation.4 | async-start | bytes 2113536 | tf_op jit(solution)/shard_map/all_gather | solution.py:64
  8.7 911.4 %reduce-scatter.3.cloned.1.call-start = ((), (), s32[]{:S(2)}) async-start(), calls=%async_computation.3 | async-start | bytes 2113536 | tf_op jit(solution)/shard_map/reduce_scatter | solution.py:52
  9.8 16.2 copy-start.4
  252.2 23.6 %copy-start.2 = (f32[2,8,256]{2,1,0:T(8,128)S(1)}, f32[2,8,256]{2,1,0:T(8,128)}, u32[]{:S(2)}) copy-start(f32[2,8,256]{2,1,0:T(8,128)} %param.16) | copy-start | bytes 49156
  252.2 25.5 %copy-start.1 = (f32[2,256,256]{2,1,0:T(8,128)S(1)}, f32[2,256,256]{2,1,0:T(8,128)}, u32[]{:S(2)}) copy-start(f32[2,256,256]{2,1,0:T(8,128)} %param.14) | copy-start | bytes 1572868
  283.4 776.6 %all-gather.8.cloned.1.call-start = ((), (), s32[]{:S(2)}) async-start(), calls=%async_computation.5 | async-start | bytes 2113536 | tf_op jit(solution)/shard_map/all_gather | solution.py:42
  283.7 224.0 %copy-start.5 = (f32[2,8,256]{2,1,0:T(8,128)S(1)}, f32[2,8,256]{2,1,0:T(8,128)}, u32[]{:S(2)}) copy-start(f32[2,8,256]{2,1,0:T(8,128)} %param.17) | copy-start | bytes 49156
  998.2 773.3 %copy-start.6 = (f32[2,8,256]{2,1,0:T(8,128)S(1)}, f32[2,8,256]{2,1,0:T(8,128)}, u32[]{:S(2)}) copy-start(f32[2,8,256]{2,1,0:T(8,128)} %param.15) | copy-start | bytes 49156
  998.9 702.5 %copy-start.3 = (f32[2,8,256]{2,1,0:T(8,128)S(1)}, f32[2,8,256]{2,1,0:T(8,128)}, u32[]{:S(2)}) copy-start(f32[2,8,256]{2,1,0:T(8,128)} %multiply_subtract_fusion) | copy-start | bytes 49156
  998.9 702.5 %reduce-scatter.5.cloned.1.call-start = ((), (), s32[]{:S(2)}) async-start(), calls=%async_computation.6 | async-start | bytes 2113536 | tf_op jit(solution)/shard_map/reduce_scatter | solution.py:52
Sparse Core Ops, SparseCore 0:
  11.2 68.9 all-gather.3
  83.3 62.7 all-gather.5
  283.5 636.5 reduce-scatter.2
  999.0 60.9 all-gather.7
  1071.3 630.0 reduce-scatter.4
